TPU v7x, 32 devices: a whole 2x2x4 slice. The times are simulated.
32 devices in a mesh: shot: 2 (over y), gx: 4 (over z), gy: 4 (over x, core).
Axes of the slice: x: 2, y: 2, z: 4, core: 2. Of those that a mesh axis runs over, the one named last changes fastest.
Arguments:
- source_prev: float32 [64, 32, 320], P(('shot', 'gx'), 'gy'), parts along dimension 0, may hold values from -0.6 to 0.6
- source_now: float32 [64, 32, 320], P(('shot', 'gx'), 'gy'), parts along dimension 0, may hold values from -0.6 to 0.6
- receiver_prev: float32 [64, 32, 320], P(('shot', 'gx'), 'gy'), parts along dimension 0, may hold values from -6 to 6
- receiver_now: float32 [64, 32, 320], P(('shot', 'gx'), 'gy'), parts along dimension 0, may hold values from -6 to 6
- speed_squared: float32 [64, 32, 320], P(('shot', 'gx'), 'gy'), parts along dimension 0, may hold values from 0.05 to 0.18
- wavelet: float32 [20], P('shot'), parts along dimension 0, may hold values from -40 to 40
- source_cell: int32 [2], P('shot'), parts along dimension 0, may hold values from 0 to 327679
- traces: float32 [20, 1024], P('shot', ('gx', 'gy')), parts along dimension 0, may hold values from -18 to 18
- receiver_cells: int32 [2, 1024], P('shot', ('gx', 'gy')), parts along dimension 0, may hold values from 0 to 1023
- plan: int32 [8], P('shot'), parts along dimension 0, may hold values from 0 to 9, as said below
- stored_snapshots: bfloat16 [8, 32, 32, 320], P('shot', 'gx', 'gy'), parts along dimension 0, may hold values from -6 to 6
- image_before: float32 [64, 32, 320], P(('shot', 'gx'), 'gy'), parts along dimension 0, may hold values from -6 to 6
Outputs:
- new_source_prev: float32 [64, 32, 320], P(('shot', 'gx'), 'gy'), parts along dimension 0
- new_source_now: float32 [64, 32, 320], P(('shot', 'gx'), 'gy'), parts along dimension 0
- new_receiver_prev: float32 [64, 32, 320], P(('shot', 'gx'), 'gy'), parts along dimension 0
- new_receiver_now: float32 [64, 32, 320], P(('shot', 'gx'), 'gy'), parts along dimension 0
- snapshots: bfloat16 [8, 32, 32, 320], P('shot', 'gx', 'gy'), parts along dimension 0
- image: float32 [64, 32, 320], P(('shot', 'gx'), 'gy'), parts along dimension 0
There are 2 independent parts, one for each index of `shot`. A program takes and returns all parts, laid end to end along the dimension named above; each array names one. Nothing has to cross between parts.
Inputs may be any that keep to these rules, and one draw needn't show every extreme that they name: `plan`: 4 different steps in increasing order; the first is 0 and the last is 9.
All inputs are finite; a program needn't handle non-finite values.
Results may differ from a plain program's by a relative error of at most 0.001.
Values sent between devices are 32-bit elements; how exact they have to be, the bound alone decides.
A program may use at most 64 MiB of HBM per device.

v0:
```python
import jax
import jax.numpy as jnp
from jax import lax
from jax.sharding import PartitionSpec as P

STENCIL_COEFFS = (-205.0 / 72.0, 8.0 / 5.0, -1.0 / 5.0, 8.0 / 315.0, -1.0 / 560.0)


def with_halo(block, sides, width):
    for axis, dim in sides:
        count = lax.axis_size(axis)
        forward = [(i, i + 1) for i in range(count - 1)]
        backward = [(target, source) for source, target in forward]
        low = lax.ppermute(
            lax.slice_in_dim(block, block.shape[dim] - width, None, axis=dim), axis, forward
        )
        high = lax.ppermute(lax.slice_in_dim(block, 0, width, axis=dim), axis, backward)
        block = jnp.concatenate([low, block, high], axis=dim)
    return block


def stencil(padded):
    span_x = padded.shape[0] - 8
    span_y = padded.shape[1] - 8
    depth_cells = padded.shape[2]
    deepened = jnp.pad(padded, ((0, 0), (0, 0), (4, 4)))

    def window(shift_x, shift_y, shift_z):
        return deepened[
            4 + shift_x : 4 + shift_x + span_x,
            4 + shift_y : 4 + shift_y + span_y,
            4 + shift_z : 4 + shift_z + depth_cells,
        ]

    summed = 3.0 * STENCIL_COEFFS[0] * window(0, 0, 0)
    for distance in range(1, 5):
        neighbours = window(distance, 0, 0) + window(-distance, 0, 0)
        neighbours = neighbours + window(0, distance, 0) + window(0, -distance, 0)
        neighbours = neighbours + window(0, 0, distance) + window(0, 0, -distance)
        summed = summed + STENCIL_COEFFS[distance] * neighbours
    return summed


def body(
    source_prev,
    source_now,
    receiver_prev,
    receiver_now,
    speed_squared,
    wavelet,
    source_cell,
    traces,
    receiver_cells,
    plan,
    stored_snapshots,
    image_before,
):
    block_x, block_y, depth_cells = source_now.shape
    grid_y = block_y * lax.axis_size("gy")
    start_x = lax.axis_index("gx") * block_x
    start_y = lax.axis_index("gy") * block_y
    total_steps = wavelet.shape[0]
    slot_count = plan.shape[0]
    border = 0
    span_x = block_x + 2 * border
    span_y = block_y + 2 * border
    plane_cells = span_x * span_y
    values = lax.all_gather(traces, ("gx", "gy"), axis=1, tiled=True)
    cell_ids = lax.all_gather(receiver_cells, ("gx", "gy"), axis=1, tiled=True)
    cell_ids = cell_ids[0]
    local_x = cell_ids // grid_y - (start_x - border)
    local_y = cell_ids % grid_y - (start_y - border)
    in_block = (local_x >= 0) & (local_x < span_x) & (local_y >= 0) & (local_y < span_y)
    local_cell = jnp.where(in_block, local_x * span_y + local_y, plane_cells)
    injected = (
        jnp.zeros((total_steps, plane_cells), jnp.float32)
        .at[:, local_cell]
        .add(values, mode="drop")
    )
    injected = injected.reshape(total_steps, span_x, span_y)
    snapshots = jnp.zeros(stored_snapshots.shape, jnp.bfloat16)
    imaged = image_before
    along_x = start_x - 0 + lax.broadcasted_iota(jnp.int32, (block_x + 2 * 0, 1, 1), 0)
    along_y = start_y - 0 + lax.broadcasted_iota(jnp.int32, (1, block_y + 2 * 0, 1), 1)
    along_x, along_y = (along_x, along_y)
    along_z = lax.broadcasted_iota(jnp.int32, (1, 1, depth_cells), 2)
    cell_id = source_cell[0]
    matches = (along_x == cell_id // (grid_y * depth_cells)) & (
        along_y == cell_id // depth_cells % grid_y
    )
    matches = matches & (along_z == cell_id % depth_cells)
    source_core = matches.astype(jnp.float32)
    source_before, source_field = (source_prev, source_now)
    receiver_before, receiver_field = (receiver_prev, receiver_now)
    for step_index in range(total_steps):
        back_time = total_steps - 1 - step_index
        padded = with_halo(jnp.stack([source_field, receiver_field]), (("gx", 1), ("gy", 2)), 4)
        source_spread = stencil(padded[0]) + wavelet[step_index] * source_core
        receiver_spread = stencil(padded[1]).at[:, :, 0].add(injected[back_time])
        source_latest = 2.0 * source_field - source_before + speed_squared * source_spread
        receiver_latest = 2.0 * receiver_field - receiver_before + speed_squared * receiver_spread
        source_before, source_field = (source_field, source_latest)
        receiver_before, receiver_field = (receiver_field, receiver_latest)
        record_matches = plan == step_index
        snapshots = jnp.where(
            record_matches[:, None, None, None], source_field.astype(jnp.bfloat16)[None], snapshots
        )
        correlate_matches = plan == back_time
        slot_index = jnp.sum(
            jnp.where(correlate_matches, jnp.arange(slot_count, dtype=jnp.int32), 0)
        )
        present = jnp.any(correlate_matches)
        snapshot = lax.dynamic_index_in_dim(stored_snapshots, slot_index, 0, keepdims=False).astype(
            jnp.float32
        )
        imaged = imaged + jnp.where(present, snapshot * receiver_field, 0.0)
    source_last, source_final = (source_before, source_field)
    previous, current = (receiver_before, receiver_field)
    return (source_last, source_final, previous, current, snapshots, imaged)


def solution(mesh):
    placed = (
        P(("shot", "gx"), "gy", None),
        P(("shot", "gx"), "gy", None),
        P(("shot", "gx"), "gy", None),
        P(("shot", "gx"), "gy", None),
        P(("shot", "gx"), "gy", None),
        P("shot"),
        P("shot"),
        P("shot", ("gx", "gy")),
        P("shot", ("gx", "gy")),
        P("shot"),
        P("shot", "gx", "gy", None),
        P(("shot", "gx"), "gy", None),
    )
    return jax.shard_map(
        body,
        mesh=mesh,
        in_specs=placed,
        out_specs=(
            P(("shot", "gx"), "gy", None),
            P(("shot", "gx"), "gy", None),
            P(("shot", "gx"), "gy", None),
            P(("shot", "gx"), "gy", None),
            P("shot", "gx", "gy", None),
            P(("shot", "gx"), "gy", None),
        ),
        check_vma=False,
    )
```

profile of v0, /device:TPU:18, one launch (start us, length us, event | category | flops | bytes accessed | tf_op | source)
XLA Modules:
  0.0 254.4 jit_solution(9579591347282151355)
XLA Ops:
  1.6 2.5 collective-permute-start.1
  4.1 3.5 %collective-permute-start = (f32[2,4,8,320]{3,2,1,0:T(8,128)S(1)}, f32[2,4,8,320]{3,2,1,0:T(8,128)S(1)}, u32[]{:S(2)}, u32[]{:S(2)}) collective-permute-start(f32[2,4,8,320]{3,2,1,0:T(8,128)S(1)} %get-tuple-element.250), channel_id=1, source_target_pairs={{0,4},{4,8},{8,12},{1,5},{5,9},{9,13},{2,6},{6,10},{10,14},{3,7},{... | collective-permute-start | bytes 245768 | tf_op jit(solution)/shard_map/ppermute | solution.py:14
  9.7 9.4 %all-reduce.20 = s32[1024]{0:T(1024)S(1)} all-reduce(s32[1024]{0:T(1024)S(1)} %bitcast_dynamic-update-slice_fusion), channel_id=1, replica_groups=mesh['shot'=2,'gx'=4,'gy'=4] {'gx','gy'}, use_global_device_ids=true, to_apply=%add.20 | all-reduce | flops 1024 | bytes 8192
  21.3 2.4 collective-permute-start.2
  23.8 15.2 %all-gather = f32[16,64,10]{1,2,0:T(8,128)S(1)} all-gather(f32[1,64,10]{1,2,0:T(8,128)S(1)} %bitcast.208), channel_id=1, replica_groups=mesh['shot'=2,'gx'=4,'gy'=4] {'gx','gy'}, dimensions={0}, use_global_device_ids=true | all-gather | bytes 43520 | tf_op jit(solution)/shard_map/all_gather | solution.py:68
  39.2 6.0 %scatter_custom_fusion = f32[10,64]{0,1:T(8,128)S(1)} fusion(s32[1024]{0:T(1024)S(1)} %bitcast.209, f32[1024,10]{1,0:T(8,128)S(1)} %bitcast.206, f32[]{:T(128)} %constant.323.clone.1), kind=kCustom, calls=%fused_computation.926 | custom fusion | flops 10240 | bytes 2564 | tf_op jit(solution)/shard_map/scatter-add | solution.py:78
  49.3 3.3 %collective-permute-start.5 = (f32[2,4,8,320]{3,2,1,0:T(8,128)S(1)}, f32[2,4,8,320]{3,2,1,0:T(8,128)S(1)}, u32[]{:S(2)}, u32[]{:S(2)}) collective-permute-start(f32[2,4,8,320]{3,2,1,0:T(8,128)S(1)} %get-tuple-element.249), channel_id=1, source_target_pairs={{4,0},{8,4},{12,8},{5,1},{9,5},{13,9},{6,2},{10,6},{14,10},{7,3},{... | collective-permute-start | bytes 245768 | tf_op jit(solution)/shard_map/ppermute | solution.py:17
  52.6 2.6 %collective-permute-start.4 = (f32[2,4,8,320]{3,2,1,0:T(8,128)S(1)}, f32[2,4,8,320]{3,2,1,0:T(8,128)S(1)}, u32[]{:S(2)}, u32[]{:S(2)}) collective-permute-start(f32[2,4,8,320]{3,2,1,0:T(8,128)S(1)} %get-tuple-element.248), channel_id=1, source_target_pairs={{0,4},{4,8},{8,12},{1,5},{5,9},{9,13},{2,6},{6,10},{10,14},{3,7},{... | collective-permute-start | bytes 245768 | tf_op jit(solution)/shard_map/ppermute | solution.py:14
  56.3 4.3 %collective-permute-done.4 = f32[2,4,8,320]{3,2,1,0:T(8,128)S(1)} collective-permute-done((f32[2,4,8,320]{3,2,1,0:T(8,128)S(1)}, f32[2,4,8,320]{3,2,1,0:T(8,128)S(1)}, u32[]{:S(2)}, u32[]{:S(2)}) %collective-permute-start.4) | collective-permute-done | bytes 81952 | tf_op jit(solution)/shard_map/ppermute | solution.py:14
  60.7 3.6 %collective-permute-start.7 = (f32[2,16,4,320]{3,1,2,0:T(8,128)S(1)}, f32[2,16,4,320]{3,1,2,0:T(8,128)S(1)}, u32[]{:S(2)}, u32[]{:S(2)}) collective-permute-start(f32[2,16,4,320]{3,1,2,0:T(8,128)S(1)} %copy.731), channel_id=1, source_target_pairs={{1,0},{2,1},{3,2},{5,4},{6,5},{7,6},{9,8},{10,9},{11,10},{13,12},{... | collective-permute-start | bytes 491528 | tf_op jit(solution)/shard_map/ppermute | solution.py:17
  67.6 3.8 %collective-permute-done.6 = f32[2,16,4,320]{3,1,2,0:T(8,128)S(1)} collective-permute-done((f32[2,16,4,320]{3,1,2,0:T(8,128)S(1)}, f32[2,16,4,320]{3,1,2,0:T(8,128)S(1)}, u32[]{:S(2)}, u32[]{:S(2)}) %collective-permute-start.6) | collective-permute-done | bytes 163872 | tf_op jit(solution)/shard_map/ppermute | solution.py:14
  73.1 3.4 %collective-permute-start.9 = (f32[2,4,8,320]{3,2,1,0:T(8,128)S(1)}, f32[2,4,8,320]{3,2,1,0:T(8,128)S(1)}, u32[]{:S(2)}, u32[]{:S(2)}) collective-permute-start(f32[2,4,8,320]{3,2,1,0:T(8,128)S(1)} %get-tuple-element.247), channel_id=1, source_target_pairs={{4,0},{8,4},{12,8},{5,1},{9,5},{13,9},{6,2},{10,6},{14,10},{7,3},{... | collective-permute-start | bytes 245768 | tf_op jit(solution)/shard_map/ppermute | solution.py:17
  76.4 2.5 collective-permute-start.8
  79.6 3.4 %collective-permute-done.8 = f32[2,4,8,320]{3,2,1,0:T(8,128)S(1)} collective-permute-done((f32[2,4,8,320]{3,2,1,0:T(8,128)S(1)}, f32[2,4,8,320]{3,2,1,0:T(8,128)S(1)}, u32[]{:S(2)}, u32[]{:S(2)}) %collective-permute-start.8) | collective-permute-done | bytes 81952 | tf_op jit(solution)/shard_map/ppermute | solution.py:14
  85.0 2.4 collective-permute-start.10
  88.2 3.8 %collective-permute-done.10 = f32[2,16,4,320]{3,1,2,0:T(8,128)S(1)} collective-permute-done((f32[2,16,4,320]{3,1,2,0:T(8,128)S(1)}, f32[2,16,4,320]{3,1,2,0:T(8,128)S(1)}, u32[]{:S(2)}, u32[]{:S(2)}) %collective-permute-start.10) | collective-permute-done | bytes 163872 | tf_op jit(solution)/shard_map/ppermute | solution.py:14
  95.7 3.9 %collective-permute-start.12 = (f32[2,4,8,320]{3,2,1,0:T(8,128)S(1)}, f32[2,4,8,320]{3,2,1,0:T(8,128)S(1)}, u32[]{:S(2)}, u32[]{:S(2)}) collective-permute-start(f32[2,4,8,320]{3,2,1,0:T(8,128)S(1)} %get-tuple-element.244), channel_id=1, source_target_pairs={{0,4},{4,8},{8,12},{1,5},{5,9},{9,13},{2,6},{6,10},{10,14},{3,7},{... | collective-permute-start | bytes 245768 | tf_op jit(solution)/shard_map/ppermute | solution.py:14
  107.5 3.8 %collective-permute-done.14 = f32[2,16,4,320]{3,1,2,0:T(8,128)S(1)} collective-permute-done((f32[2,16,4,320]{3,1,2,0:T(8,128)S(1)}, f32[2,16,4,320]{3,1,2,0:T(8,128)S(1)}, u32[]{:S(2)}, u32[]{:S(2)}) %collective-permute-start.14) | collective-permute-done | bytes 163872 | tf_op jit(solution)/shard_map/ppermute | solution.py:14
  114.9 3.9 %collective-permute-start.16 = (f32[2,4,8,320]{3,2,1,0:T(8,128)S(1)}, f32[2,4,8,320]{3,2,1,0:T(8,128)S(1)}, u32[]{:S(2)}, u32[]{:S(2)}) collective-permute-start(f32[2,4,8,320]{3,2,1,0:T(8,128)S(1)} %get-tuple-element.242), channel_id=1, source_target_pairs={{0,4},{4,8},{8,12},{1,5},{5,9},{9,13},{2,6},{6,10},{10,14},{3,7},{... | collective-permute-start | bytes 245768 | tf_op jit(solution)/shard_map/ppermute | solution.py:14
  126.7 3.8 %collective-permute-done.18 = f32[2,16,4,320]{3,1,2,0:T(8,128)S(1)} collective-permute-done((f32[2,16,4,320]{3,1,2,0:T(8,128)S(1)}, f32[2,16,4,320]{3,1,2,0:T(8,128)S(1)}, u32[]{:S(2)}, u32[]{:S(2)}) %collective-permute-start.18) | collective-permute-done | bytes 163872 | tf_op jit(solution)/shard_map/ppermute | solution.py:14
  134.2 3.9 %collective-permute-start.20 = (f32[2,4,8,320]{3,2,1,0:T(8,128)S(1)}, f32[2,4,8,320]{3,2,1,0:T(8,128)S(1)}, u32[]{:S(2)}, u32[]{:S(2)}) collective-permute-start(f32[2,4,8,320]{3,2,1,0:T(8,128)S(1)} %get-tuple-element.240), channel_id=1, source_target_pairs={{0,4},{4,8},{8,12},{1,5},{5,9},{9,13},{2,6},{6,10},{10,14},{3,7},{... | collective-permute-start | bytes 245768 | tf_op jit(solution)/shard_map/ppermute | solution.py:14
  142.7 2.6 %collective-permute-start.22 = (f32[2,16,4,320]{3,1,2,0:T(8,128)S(1)}, f32[2,16,4,320]{3,1,2,0:T(8,128)S(1)}, u32[]{:S(2)}, u32[]{:S(2)}) collective-permute-start(f32[2,16,4,320]{3,1,2,0:T(8,128)S(1)} %copy.738), channel_id=1, source_target_pairs={{0,1},{1,2},{2,3},{4,5},{5,6},{6,7},{8,9},{9,10},{10,11},{12,13},{... | collective-permute-start | bytes 491528 | tf_op jit(solution)/shard_map/ppermute | solution.py:14
  146.0 3.8 %collective-permute-done.22 = f32[2,16,4,320]{3,1,2,0:T(8,128)S(1)} collective-permute-done((f32[2,16,4,320]{3,1,2,0:T(8,128)S(1)}, f32[2,16,4,320]{3,1,2,0:T(8,128)S(1)}, u32[]{:S(2)}, u32[]{:S(2)}) %collective-permute-start.22) | collective-permute-done | bytes 163872 | tf_op jit(solution)/shard_map/ppermute | solution.py:14
  153.4 3.9 %collective-permute-start.24 = (f32[2,4,8,320]{3,2,1,0:T(8,128)S(1)}, f32[2,4,8,320]{3,2,1,0:T(8,128)S(1)}, u32[]{:S(2)}, u32[]{:S(2)}) collective-permute-start(f32[2,4,8,320]{3,2,1,0:T(8,128)S(1)} %get-tuple-element.238), channel_id=1, source_target_pairs={{0,4},{4,8},{8,12},{1,5},{5,9},{9,13},{2,6},{6,10},{10,14},{3,7},{... | collective-permute-start | bytes 245768 | tf_op jit(solution)/shard_map/ppermute | solution.py:14
  165.2 3.8 %collective-permute-done.26 = f32[2,16,4,320]{3,1,2,0:T(8,128)S(1)} collective-permute-done((f32[2,16,4,320]{3,1,2,0:T(8,128)S(1)}, f32[2,16,4,320]{3,1,2,0:T(8,128)S(1)}, u32[]{:S(2)}, u32[]{:S(2)}) %collective-permute-start.26) | collective-permute-done | bytes 163872 | tf_op jit(solution)/shard_map/ppermute | solution.py:14
  172.7 3.9 %collective-permute-start.28 = (f32[2,4,8,320]{3,2,1,0:T(8,128)S(1)}, f32[2,4,8,320]{3,2,1,0:T(8,128)S(1)}, u32[]{:S(2)}, u32[]{:S(2)}) collective-permute-start(f32[2,4,8,320]{3,2,1,0:T(8,128)S(1)} %get-tuple-element.236), channel_id=1, source_target_pairs={{0,4},{4,8},{8,12},{1,5},{5,9},{9,13},{2,6},{6,10},{10,14},{3,7},{... | collective-permute-start | bytes 245768 | tf_op jit(solution)/shard_map/ppermute | solution.py:14
  184.5 3.8 %collective-permute-done.30 = f32[2,16,4,320]{3,1,2,0:T(8,128)S(1)} collective-permute-done((f32[2,16,4,320]{3,1,2,0:T(8,128)S(1)}, f32[2,16,4,320]{3,1,2,0:T(8,128)S(1)}, u32[]{:S(2)}, u32[]{:S(2)}) %collective-permute-start.30) | collective-permute-done | bytes 163872 | tf_op jit(solution)/shard_map/ppermute | solution.py:14
  191.9 3.9 %collective-permute-start.32 = (f32[2,4,8,320]{3,2,1,0:T(8,128)S(1)}, f32[2,4,8,320]{3,2,1,0:T(8,128)S(1)}, u32[]{:S(2)}, u32[]{:S(2)}) collective-permute-start(f32[2,4,8,320]{3,2,1,0:T(8,128)S(1)} %get-tuple-element.234), channel_id=1, source_target_pairs={{0,4},{4,8},{8,12},{1,5},{5,9},{9,13},{2,6},{6,10},{10,14},{3,7},{... | collective-permute-start | bytes 245768 | tf_op jit(solution)/shard_map/ppermute | solution.py:14
  203.8 3.8 %collective-permute-done.34 = f32[2,16,4,320]{3,1,2,0:T(8,128)S(1)} collective-permute-done((f32[2,16,4,320]{3,1,2,0:T(8,128)S(1)}, f32[2,16,4,320]{3,1,2,0:T(8,128)S(1)}, u32[]{:S(2)}, u32[]{:S(2)}) %collective-permute-start.34) | collective-permute-done | bytes 163872 | tf_op jit(solution)/shard_map/ppermute | solution.py:14
  211.4 3.9 %collective-permute-start.36 = (f32[2,4,8,320]{3,2,1,0:T(8,128)S(1)}, f32[2,4,8,320]{3,2,1,0:T(8,128)S(1)}, u32[]{:S(2)}, u32[]{:S(2)}) collective-permute-start(f32[2,4,8,320]{3,2,1,0:T(8,128)S(1)} %get-tuple-element.232), channel_id=1, source_target_pairs={{0,4},{4,8},{8,12},{1,5},{5,9},{9,13},{2,6},{6,10},{10,14},{3,7},{... | collective-permute-start | bytes 245768 | tf_op jit(solution)/shard_map/ppermute | solution.py:14
  240.4 3.7 %collective-permute-done.38 = f32[2,16,4,320]{3,1,2,0:T(8,128)S(1)} collective-permute-done((f32[2,16,4,320]{3,1,2,0:T(8,128)S(1)}, f32[2,16,4,320]{3,1,2,0:T(8,128)S(1)}, u32[]{:S(2)}, u32[]{:S(2)}) %collective-permute-start.38) | collective-permute-done | bytes 163872 | tf_op jit(solution)/shard_map/ppermute | solution.py:14
  247.3 7.1 %fusion.361 = (f32[8,8,320]{2,1,0:T(8,128)}, f32[8,8,320]{2,1,0:T(8,128)}) fusion(f32[8,8,320]{2,1,0:T(8,128)S(1)} %multiply_add_fusion.1, f32[8,8,320]{2,1,0:T(8,128)S(1)} %multiply_add_fusion.3, f32[8,8,320]{2,1,0:T(8,128)S(1)} %multiply_add_fusion.4, f32[8,8,320]{2,1,0:T(8,128)S(1)} %multiply_add_fusion.8, f32[8,8,320]{2,1,0:T(8,128)S(1)} %copy-done.7, ...), kind=kLoop, calls=%fused_computation.864 | loop fusion | flops 1228800 | bytes 1556530 | tf_op jit(solution)/shard_map/add | solution.py:116
  (231 shorter events, 96.8 us)
Async XLA Ops:
  1.6 17.6 %collective-permute-start.1 = (f32[2,4,8,320]{3,2,1,0:T(8,128)S(1)}, f32[2,4,8,320]{3,2,1,0:T(8,128)S(1)}, u32[]{:S(2)}, u32[]{:S(2)}) collective-permute-start(f32[2,4,8,320]{3,2,1,0:T(8,128)S(1)} %get-tuple-element.251), channel_id=1, source_target_pairs={{4,0},{8,4},{12,8},{5,1},{9,5},{13,9},{6,2},{10,6},{14,10},{7,3},{... | collective-permute-start | bytes 245768 | tf_op jit(solution)/shard_map/ppermute | solution.py:17
  4.1 15.1 %collective-permute-start = (f32[2,4,8,320]{3,2,1,0:T(8,128)S(1)}, f32[2,4,8,320]{3,2,1,0:T(8,128)S(1)}, u32[]{:S(2)}, u32[]{:S(2)}) collective-permute-start(f32[2,4,8,320]{3,2,1,0:T(8,128)S(1)} %get-tuple-element.250), channel_id=1, source_target_pairs={{0,4},{4,8},{8,12},{1,5},{5,9},{9,13},{2,6},{6,10},{10,14},{3,7},{... | collective-permute-start | bytes 245768 | tf_op jit(solution)/shard_map/ppermute | solution.py:14
  19.3 26.6 %collective-permute-start.3 = (f32[2,16,4,320]{3,1,2,0:T(8,128)S(1)}, f32[2,16,4,320]{3,1,2,0:T(8,128)S(1)}, u32[]{:S(2)}, u32[]{:S(2)}) collective-permute-start(f32[2,16,4,320]{3,1,2,0:T(8,128)S(1)} %copy.729), channel_id=1, source_target_pairs={{1,0},{2,1},{3,2},{5,4},{6,5},{7,6},{9,8},{10,9},{11,10},{13,12},{... | collective-permute-start | bytes 491528 | tf_op jit(solution)/shard_map/ppermute | solution.py:17
  21.3 24.7 %collective-permute-start.2 = (f32[2,16,4,320]{3,1,2,0:T(8,128)S(1)}, f32[2,16,4,320]{3,1,2,0:T(8,128)S(1)}, u32[]{:S(2)}, u32[]{:S(2)}) collective-permute-start(f32[2,16,4,320]{3,1,2,0:T(8,128)S(1)} %copy.728), channel_id=1, source_target_pairs={{0,1},{1,2},{2,3},{4,5},{5,6},{6,7},{8,9},{9,10},{10,11},{12,13},{... | collective-permute-start | bytes 491528 | tf_op jit(solution)/shard_map/ppermute | solution.py:14
  49.3 6.9 %collective-permute-start.5 = (f32[2,4,8,320]{3,2,1,0:T(8,128)S(1)}, f32[2,4,8,320]{3,2,1,0:T(8,128)S(1)}, u32[]{:S(2)}, u32[]{:S(2)}) collective-permute-start(f32[2,4,8,320]{3,2,1,0:T(8,128)S(1)} %get-tuple-element.249), channel_id=1, source_target_pairs={{4,0},{8,4},{12,8},{5,1},{9,5},{13,9},{6,2},{10,6},{14,10},{7,3},{... | collective-permute-start | bytes 245768 | tf_op jit(solution)/shard_map/ppermute | solution.py:17
  52.6 8.0 %collective-permute-start.4 = (f32[2,4,8,320]{3,2,1,0:T(8,128)S(1)}, f32[2,4,8,320]{3,2,1,0:T(8,128)S(1)}, u32[]{:S(2)}, u32[]{:S(2)}) collective-permute-start(f32[2,4,8,320]{3,2,1,0:T(8,128)S(1)} %get-tuple-element.248), channel_id=1, source_target_pairs={{0,4},{4,8},{8,12},{1,5},{5,9},{9,13},{2,6},{6,10},{10,14},{3,7},{... | collective-permute-start | bytes 245768 | tf_op jit(solution)/shard_map/ppermute | solution.py:14
  60.7 6.8 %collective-permute-start.7 = (f32[2,16,4,320]{3,1,2,0:T(8,128)S(1)}, f32[2,16,4,320]{3,1,2,0:T(8,128)S(1)}, u32[]{:S(2)}, u32[]{:S(2)}) collective-permute-start(f32[2,16,4,320]{3,1,2,0:T(8,128)S(1)} %copy.731), channel_id=1, source_target_pairs={{1,0},{2,1},{3,2},{5,4},{6,5},{7,6},{9,8},{10,9},{11,10},{13,12},{... | collective-permute-start | bytes 491528 | tf_op jit(solution)/shard_map/ppermute | solution.py:17
  64.4 7.0 %collective-permute-start.6 = (f32[2,16,4,320]{3,1,2,0:T(8,128)S(1)}, f32[2,16,4,320]{3,1,2,0:T(8,128)S(1)}, u32[]{:S(2)}, u32[]{:S(2)}) collective-permute-start(f32[2,16,4,320]{3,1,2,0:T(8,128)S(1)} %copy.730), channel_id=1, source_target_pairs={{0,1},{1,2},{2,3},{4,5},{5,6},{6,7},{8,9},{9,10},{10,11},{12,13},{... | collective-permute-start | bytes 491528 | tf_op jit(solution)/shard_map/ppermute | solution.py:14
  73.1 6.5 %collective-permute-start.9 = (f32[2,4,8,320]{3,2,1,0:T(8,128)S(1)}, f32[2,4,8,320]{3,2,1,0:T(8,128)S(1)}, u32[]{:S(2)}, u32[]{:S(2)}) collective-permute-start(f32[2,4,8,320]{3,2,1,0:T(8,128)S(1)} %get-tuple-element.247), channel_id=1, source_target_pairs={{4,0},{8,4},{12,8},{5,1},{9,5},{13,9},{6,2},{10,6},{14,10},{7,3},{... | collective-permute-start | bytes 245768 | tf_op jit(solution)/shard_map/ppermute | solution.py:17
  76.4 6.5 %collective-permute-start.8 = (f32[2,4,8,320]{3,2,1,0:T(8,128)S(1)}, f32[2,4,8,320]{3,2,1,0:T(8,128)S(1)}, u32[]{:S(2)}, u32[]{:S(2)}) collective-permute-start(f32[2,4,8,320]{3,2,1,0:T(8,128)S(1)} %get-tuple-element.246), channel_id=1, source_target_pairs={{0,4},{4,8},{8,12},{1,5},{5,9},{9,13},{2,6},{6,10},{10,14},{3,7},{... | collective-permute-start | bytes 245768 | tf_op jit(solution)/shard_map/ppermute | solution.py:14
  85.0 7.0 %collective-permute-start.10 = (f32[2,16,4,320]{3,1,2,0:T(8,128)S(1)}, f32[2,16,4,320]{3,1,2,0:T(8,128)S(1)}, u32[]{:S(2)}, u32[]{:S(2)}) collective-permute-start(f32[2,16,4,320]{3,1,2,0:T(8,128)S(1)} %copy.732), channel_id=1, source_target_pairs={{0,1},{1,2},{2,3},{4,5},{5,6},{6,7},{8,9},{9,10},{10,11},{12,13},{... | collective-permute-start | bytes 491528 | tf_op jit(solution)/shard_map/ppermute | solution.py:14
  93.7 6.5 %collective-permute-start.13 = (f32[2,4,8,320]{3,2,1,0:T(8,128)S(1)}, f32[2,4,8,320]{3,2,1,0:T(8,128)S(1)}, u32[]{:S(2)}, u32[]{:S(2)}) collective-permute-start(f32[2,4,8,320]{3,2,1,0:T(8,128)S(1)} %get-tuple-element.245), channel_id=1, source_target_pairs={{4,0},{8,4},{12,8},{5,1},{9,5},{13,9},{6,2},{10,6},{14,10},{7,3},{... | collective-permute-start | bytes 245768 | tf_op jit(solution)/shard_map/ppermute | solution.py:17
  95.7 6.5 %collective-permute-start.12 = (f32[2,4,8,320]{3,2,1,0:T(8,128)S(1)}, f32[2,4,8,320]{3,2,1,0:T(8,128)S(1)}, u32[]{:S(2)}, u32[]{:S(2)}) collective-permute-start(f32[2,4,8,320]{3,2,1,0:T(8,128)S(1)} %get-tuple-element.244), channel_id=1, source_target_pairs={{0,4},{4,8},{8,12},{1,5},{5,9},{9,13},{2,6},{6,10},{10,14},{3,7},{... | collective-permute-start | bytes 245768 | tf_op jit(solution)/shard_map/ppermute | solution.py:14
  104.2 7.0 %collective-permute-start.14 = (f32[2,16,4,320]{3,1,2,0:T(8,128)S(1)}, f32[2,16,4,320]{3,1,2,0:T(8,128)S(1)}, u32[]{:S(2)}, u32[]{:S(2)}) collective-permute-start(f32[2,16,4,320]{3,1,2,0:T(8,128)S(1)} %copy.734), channel_id=1, source_target_pairs={{0,1},{1,2},{2,3},{4,5},{5,6},{6,7},{8,9},{9,10},{10,11},{12,13},{... | collective-permute-start | bytes 491528 | tf_op jit(solution)/shard_map/ppermute | solution.py:14
  113.0 6.5 %collective-permute-start.17 = (f32[2,4,8,320]{3,2,1,0:T(8,128)S(1)}, f32[2,4,8,320]{3,2,1,0:T(8,128)S(1)}, u32[]{:S(2)}, u32[]{:S(2)}) collective-permute-start(f32[2,4,8,320]{3,2,1,0:T(8,128)S(1)} %get-tuple-element.243), channel_id=1, source_target_pairs={{4,0},{8,4},{12,8},{5,1},{9,5},{13,9},{6,2},{10,6},{14,10},{7,3},{... | collective-permute-start | bytes 245768 | tf_op jit(solution)/shard_map/ppermute | solution.py:17
  114.9 6.5 %collective-permute-start.16 = (f32[2,4,8,320]{3,2,1,0:T(8,128)S(1)}, f32[2,4,8,320]{3,2,1,0:T(8,128)S(1)}, u32[]{:S(2)}, u32[]{:S(2)}) collective-permute-start(f32[2,4,8,320]{3,2,1,0:T(8,128)S(1)} %get-tuple-element.242), channel_id=1, source_target_pairs={{0,4},{4,8},{8,12},{1,5},{5,9},{9,13},{2,6},{6,10},{10,14},{3,7},{... | collective-permute-start | bytes 245768 | tf_op jit(solution)/shard_map/ppermute | solution.py:14
  123.5 7.0 %collective-permute-start.18 = (f32[2,16,4,320]{3,1,2,0:T(8,128)S(1)}, f32[2,16,4,320]{3,1,2,0:T(8,128)S(1)}, u32[]{:S(2)}, u32[]{:S(2)}) collective-permute-start(f32[2,16,4,320]{3,1,2,0:T(8,128)S(1)} %copy.736), channel_id=1, source_target_pairs={{0,1},{1,2},{2,3},{4,5},{5,6},{6,7},{8,9},{9,10},{10,11},{12,13},{... | collective-permute-start | bytes 491528 | tf_op jit(solution)/shard_map/ppermute | solution.py:14
  132.2 6.5 %collective-permute-start.21 = (f32[2,4,8,320]{3,2,1,0:T(8,128)S(1)}, f32[2,4,8,320]{3,2,1,0:T(8,128)S(1)}, u32[]{:S(2)}, u32[]{:S(2)}) collective-permute-start(f32[2,4,8,320]{3,2,1,0:T(8,128)S(1)} %get-tuple-element.241), channel_id=1, source_target_pairs={{4,0},{8,4},{12,8},{5,1},{9,5},{13,9},{6,2},{10,6},{14,10},{7,3},{... | collective-permute-start | bytes 245768 | tf_op jit(solution)/shard_map/ppermute | solution.py:17
  134.2 6.5 %collective-permute-start.20 = (f32[2,4,8,320]{3,2,1,0:T(8,128)S(1)}, f32[2,4,8,320]{3,2,1,0:T(8,128)S(1)}, u32[]{:S(2)}, u32[]{:S(2)}) collective-permute-start(f32[2,4,8,320]{3,2,1,0:T(8,128)S(1)} %get-tuple-element.240), channel_id=1, source_target_pairs={{0,4},{4,8},{8,12},{1,5},{5,9},{9,13},{2,6},{6,10},{10,14},{3,7},{... | collective-permute-start | bytes 245768 | tf_op jit(solution)/shard_map/ppermute | solution.py:14
  142.7 7.0 %collective-permute-start.22 = (f32[2,16,4,320]{3,1,2,0:T(8,128)S(1)}, f32[2,16,4,320]{3,1,2,0:T(8,128)S(1)}, u32[]{:S(2)}, u32[]{:S(2)}) collective-permute-start(f32[2,16,4,320]{3,1,2,0:T(8,128)S(1)} %copy.738), channel_id=1, source_target_pairs={{0,1},{1,2},{2,3},{4,5},{5,6},{6,7},{8,9},{9,10},{10,11},{12,13},{... | collective-permute-start | bytes 491528 | tf_op jit(solution)/shard_map/ppermute | solution.py:14
  151.5 6.5 %collective-permute-start.25 = (f32[2,4,8,320]{3,2,1,0:T(8,128)S(1)}, f32[2,4,8,320]{3,2,1,0:T(8,128)S(1)}, u32[]{:S(2)}, u32[]{:S(2)}) collective-permute-start(f32[2,4,8,320]{3,2,1,0:T(8,128)S(1)} %get-tuple-element.239), channel_id=1, source_target_pairs={{4,0},{8,4},{12,8},{5,1},{9,5},{13,9},{6,2},{10,6},{14,10},{7,3},{... | collective-permute-start | bytes 245768 | tf_op jit(solution)/shard_map/ppermute | solution.py:17
  153.4 6.5 %collective-permute-start.24 = (f32[2,4,8,320]{3,2,1,0:T(8,128)S(1)}, f32[2,4,8,320]{3,2,1,0:T(8,128)S(1)}, u32[]{:S(2)}, u32[]{:S(2)}) collective-permute-start(f32[2,4,8,320]{3,2,1,0:T(8,128)S(1)} %get-tuple-element.238), channel_id=1, source_target_pairs={{0,4},{4,8},{8,12},{1,5},{5,9},{9,13},{2,6},{6,10},{10,14},{3,7},{... | collective-permute-start | bytes 245768 | tf_op jit(solution)/shard_map/ppermute | solution.py:14
  162.0 7.0 %collective-permute-start.26 = (f32[2,16,4,320]{3,1,2,0:T(8,128)S(1)}, f32[2,16,4,320]{3,1,2,0:T(8,128)S(1)}, u32[]{:S(2)}, u32[]{:S(2)}) collective-permute-start(f32[2,16,4,320]{3,1,2,0:T(8,128)S(1)} %copy.740), channel_id=1, source_target_pairs={{0,1},{1,2},{2,3},{4,5},{5,6},{6,7},{8,9},{9,10},{10,11},{12,13},{... | collective-permute-start | bytes 491528 | tf_op jit(solution)/shard_map/ppermute | solution.py:14
  170.8 6.5 %collective-permute-start.29 = (f32[2,4,8,320]{3,2,1,0:T(8,128)S(1)}, f32[2,4,8,320]{3,2,1,0:T(8,128)S(1)}, u32[]{:S(2)}, u32[]{:S(2)}) collective-permute-start(f32[2,4,8,320]{3,2,1,0:T(8,128)S(1)} %get-tuple-element.237), channel_id=1, source_target_pairs={{4,0},{8,4},{12,8},{5,1},{9,5},{13,9},{6,2},{10,6},{14,10},{7,3},{... | collective-permute-start | bytes 245768 | tf_op jit(solution)/shard_map/ppermute | solution.py:17
  172.7 6.5 %collective-permute-start.28 = (f32[2,4,8,320]{3,2,1,0:T(8,128)S(1)}, f32[2,4,8,320]{3,2,1,0:T(8,128)S(1)}, u32[]{:S(2)}, u32[]{:S(2)}) collective-permute-start(f32[2,4,8,320]{3,2,1,0:T(8,128)S(1)} %get-tuple-element.236), channel_id=1, source_target_pairs={{0,4},{4,8},{8,12},{1,5},{5,9},{9,13},{2,6},{6,10},{10,14},{3,7},{... | collective-permute-start | bytes 245768 | tf_op jit(solution)/shard_map/ppermute | solution.py:14
  181.3 7.0 %collective-permute-start.30 = (f32[2,16,4,320]{3,1,2,0:T(8,128)S(1)}, f32[2,16,4,320]{3,1,2,0:T(8,128)S(1)}, u32[]{:S(2)}, u32[]{:S(2)}) collective-permute-start(f32[2,16,4,320]{3,1,2,0:T(8,128)S(1)} %copy.742), channel_id=1, source_target_pairs={{0,1},{1,2},{2,3},{4,5},{5,6},{6,7},{8,9},{9,10},{10,11},{12,13},{... | collective-permute-start | bytes 491528 | tf_op jit(solution)/shard_map/ppermute | solution.py:14
  190.0 6.5 %collective-permute-start.33 = (f32[2,4,8,320]{3,2,1,0:T(8,128)S(1)}, f32[2,4,8,320]{3,2,1,0:T(8,128)S(1)}, u32[]{:S(2)}, u32[]{:S(2)}) collective-permute-start(f32[2,4,8,320]{3,2,1,0:T(8,128)S(1)} %get-tuple-element.235), channel_id=1, source_target_pairs={{4,0},{8,4},{12,8},{5,1},{9,5},{13,9},{6,2},{10,6},{14,10},{7,3},{... | collective-permute-start | bytes 245768 | tf_op jit(solution)/shard_map/ppermute | solution.py:17
  191.9 6.5 %collective-permute-start.32 = (f32[2,4,8,320]{3,2,1,0:T(8,128)S(1)}, f32[2,4,8,320]{3,2,1,0:T(8,128)S(1)}, u32[]{:S(2)}, u32[]{:S(2)}) collective-permute-start(f32[2,4,8,320]{3,2,1,0:T(8,128)S(1)} %get-tuple-element.234), channel_id=1, source_target_pairs={{0,4},{4,8},{8,12},{1,5},{5,9},{9,13},{2,6},{6,10},{10,14},{3,7},{... | collective-permute-start | bytes 245768 | tf_op jit(solution)/shard_map/ppermute | solution.py:14
  200.5 7.0 %collective-permute-start.34 = (f32[2,16,4,320]{3,1,2,0:T(8,128)S(1)}, f32[2,16,4,320]{3,1,2,0:T(8,128)S(1)}, u32[]{:S(2)}, u32[]{:S(2)}) collective-permute-start(f32[2,16,4,320]{3,1,2,0:T(8,128)S(1)} %copy.744), channel_id=1, source_target_pairs={{0,1},{1,2},{2,3},{4,5},{5,6},{6,7},{8,9},{9,10},{10,11},{12,13},{... | collective-permute-start | bytes 491528 | tf_op jit(solution)/shard_map/ppermute | solution.py:14
  209.3 25.6 %collective-permute-start.37 = (f32[2,4,8,320]{3,2,1,0:T(8,128)S(1)}, f32[2,4,8,320]{3,2,1,0:T(8,128)S(1)}, u32[]{:S(2)}, u32[]{:S(2)}) collective-permute-start(f32[2,4,8,320]{3,2,1,0:T(8,128)S(1)} %get-tuple-element.233), channel_id=1, source_target_pairs={{4,0},{8,4},{12,8},{5,1},{9,5},{13,9},{6,2},{10,6},{14,10},{7,3},{... | collective-permute-start | bytes 245768 | tf_op jit(solution)/shard_map/ppermute | solution.py:17
  211.4 23.6 %collective-permute-start.36 = (f32[2,4,8,320]{3,2,1,0:T(8,128)S(1)}, f32[2,4,8,320]{3,2,1,0:T(8,128)S(1)}, u32[]{:S(2)}, u32[]{:S(2)}) collective-permute-start(f32[2,4,8,320]{3,2,1,0:T(8,128)S(1)} %get-tuple-element.232), channel_id=1, source_target_pairs={{0,4},{4,8},{8,12},{1,5},{5,9},{9,13},{2,6},{6,10},{10,14},{3,7},{... | collective-permute-start | bytes 245768 | tf_op jit(solution)/shard_map/ppermute | solution.py:14
  237.1 7.0 %collective-permute-start.38 = (f32[2,16,4,320]{3,1,2,0:T(8,128)S(1)}, f32[2,16,4,320]{3,1,2,0:T(8,128)S(1)}, u32[]{:S(2)}, u32[]{:S(2)}) collective-permute-start(f32[2,16,4,320]{3,1,2,0:T(8,128)S(1)} %copy.746), channel_id=1, source_target_pairs={{0,1},{1,2},{2,3},{4,5},{5,6},{6,7},{8,9},{9,10},{10,11},{12,13},{... | collective-permute-start | bytes 491528 | tf_op jit(solution)/shard_map/ppermute | solution.py:14
  (22 other events, 187.4 us)
where the time goes:
time: 256 us; the launch traced here: 254 us
  starting transfers between devices  103 us (40%)
  waiting for transfers between devices  64.8 us (25%)
  other arithmetic  32.2 us (13%)
  blocking collectives  24.6 us (10%)
  between operations  22.2 us (9%)
  local copies, waits for them, and re-layouts  7.13 us (3%)
    ppermute x20, starting transfers between devices, with_halo(): lax.ppermute(lax.slice_in_dim(block, block.shape[dim] - width, None, axis...  59.8 us
    ppermute x20, waiting for transfers between devices, with_halo(): lax.ppermute(lax.slice_in_dim(block, block.shape[dim] - width, None, axis...  53 us
    ppermute x20, starting transfers between devices, with_halo(): lax.ppermute(lax.slice_in_dim(block, 0, width, axis=dim), axis, backward)  43.6 us
    all_gather x1, blocking collectives, body(): values = lax.all_gather(traces, ('gx', 'gy'), axis=1, tiled=True)  15.2 us
    ppermute x20, waiting for transfers between devices, with_halo(): lax.ppermute(lax.slice_in_dim(block, 0, width, axis=dim), axis, backward)  11.7 us
    convert_element_type x10, other arithmetic, body(): source_field.astype(jnp.bfloat16)[None]  9.89 us
    unnamed x1, blocking collectives  9.37 us
    add x1, other arithmetic, body(): imaged = imaged + jnp.where(present, snapshot * receiver_field, 0.0)  7.05 us
  transfers between devices with their start and end apart: 40, of which 33 were waited for; matrix products, arithmetic and copies ran while one was open for 4% of the time, Pallas kernels for 0%

commit v1 on v0

--- a/solution.py
+++ b/solution.py
@@ -65,7 +65,15 @@
     span_x = block_x + 2 * border
     span_y = block_y + 2 * border
     plane_cells = span_x * span_y
-    values = lax.all_gather(traces, ("gx", "gy"), axis=1, tiled=True)
+    ways, here, lap = (lax.axis_size(("gx", "gy")), lax.axis_index(("gx", "gy")), traces.shape[1])
+    line, have = (traces, 1)
+    while have < ways:
+        line = jnp.concatenate(
+            [line, lax.ppermute(line, ("gx", "gy"), [(d, (d - have) % ways) for d in range(ways)])],
+            axis=1,
+        )
+        have = 2 * have
+    values = jnp.roll(line, here * lap, axis=1)
     cell_ids = lax.all_gather(receiver_cells, ("gx", "gy"), axis=1, tiled=True)
     cell_ids = cell_ids[0]
     local_x = cell_ids // grid_y - (start_x - border)

time: 256 us -> 250 us (0.977)
  blocking collectives: 24.6 us -> 9.37 us
  starting transfers between devices: 103 us -> 108 us
  waiting for transfers between devices: 64.8 us -> 68.4 us
    all_gather x1 -> x0, blocking collectives: 15.2 us -> none  [body(): values = lax.all_gather(traces, ('gx', 'gy'), axis=1, tiled=True)]
    ppermute x0 -> x4, waiting for transfers between devices: none -> 6.28 us  [body(): lax.ppermute(line, ('gx', 'gy'), [(d, (d - have) % ways) for d in range(w...]
    ppermute x0 -> x4, starting transfers between devices: none -> 4.79 us  [body(): lax.ppermute(line, ('gx', 'gy'), [(d, (d - have) % ways) for d in range(w...]
  transfers between devices with their start and end apart: 40 -> 44, of which waited for: 33 -> 35; matrix products, arithmetic and copies ran while one was open for 4% -> 4% of each run, Pallas kernels for 0% -> 0%
where the time goes in v1:
time: 250 us; the launch traced here: 248 us
  starting transfers between devices  108 us (43%)
  waiting for transfers between devices  68.4 us (27%)
  other arithmetic  32.4 us (13%)
  between operations  22.2 us (9%)
  blocking collectives  9.37 us (4%)
  local copies, waits for them, and re-layouts  7.91 us (3%)
    ppermute x20, starting transfers between devices, with_halo(): lax.ppermute(lax.slice_in_dim(block, block.shape[dim] - width, None, axis...  61 us
    ppermute x20, waiting for transfers between devices, with_halo(): lax.ppermute(lax.slice_in_dim(block, block.shape[dim] - width, None, axis...  51.7 us
    ppermute x20, starting transfers between devices, with_halo(): lax.ppermute(lax.slice_in_dim(block, 0, width, axis=dim), axis, backward)  42.2 us
    ppermute x20, waiting for transfers between devices, with_halo(): lax.ppermute(lax.slice_in_dim(block, 0, width, axis=dim), axis, backward)  10.4 us
    convert_element_type x10, other arithmetic, body(): source_field.astype(jnp.bfloat16)[None]  9.9 us
    unnamed x1, blocking collectives  9.37 us
    add x1, other arithmetic, body(): imaged = imaged + jnp.where(present, snapshot * receiver_field, 0.0)  7.04 us
    ppermute x4, waiting for transfers between devices, body(): lax.ppermute(line, ('gx', 'gy'), [(d, (d - have) % ways) for d in range(w...  6.28 us
  transfers between devices with their start and end apart: 44, of which 35 were waited for; matrix products, arithmetic and copies ran while one was open for 4% of the time, Pallas kernels for 0%

profile of v1, /device:TPU:18, one launch (start us, length us, event | category | flops | bytes accessed | tf_op | source)
XLA Modules:
  0.0 248.4 jit_solution(18370803998945440927)
XLA Ops:
  3.9 3.5 %collective-permute-start = (f32[2,4,8,320]{3,2,1,0:T(8,128)S(1)}, f32[2,4,8,320]{3,2,1,0:T(8,128)S(1)}, u32[]{:S(2)}, u32[]{:S(2)}) collective-permute-start(f32[2,4,8,320]{3,2,1,0:T(8,128)S(1)} %get-tuple-element.250), channel_id=1, source_target_pairs={{0,4},{4,8},{8,12},{1,5},{5,9},{9,13},{2,6},{6,10},{10,14},{3,7},{... | collective-permute-start | bytes 245768 | tf_op jit(solution)/shard_map/ppermute | solution.py:14
  10.2 9.4 %all-reduce.20 = s32[1024]{0:T(1024)S(1)} all-reduce(s32[1024]{0:T(1024)S(1)} %bitcast_dynamic-update-slice_fusion), channel_id=1, replica_groups=mesh['shot'=2,'gx'=4,'gy'=4] {'gx','gy'}, use_global_device_ids=true, to_apply=%add.20 | all-reduce | flops 1024 | bytes 8192
  21.0 3.3 %collective-permute-done.5 = f32[10,128]{1,0:T(8,128)S(1)} collective-permute-done((f32[10,128]{1,0:T(8,128)S(1)}, f32[10,128]{1,0:T(8,128)S(1)}, u32[]{:S(2)}, u32[]{:S(2)}) %collective-permute-start.5) | collective-permute-done | bytes 5152 | tf_op jit(solution)/shard_map/ppermute | solution.py:72
  26.7 3.0 %collective-permute-done.6 = f32[10,256]{1,0:T(8,128)S(1)} collective-permute-done((f32[10,256]{1,0:T(8,128)S(1)}, f32[10,256]{1,0:T(8,128)S(1)}, u32[]{:S(2)}, u32[]{:S(2)}) %collective-permute-start.6) | collective-permute-done | bytes 10272 | tf_op jit(solution)/shard_map/ppermute | solution.py:72
  33.8 2.4 collective-permute-start.2
  36.6 6.0 %scatter_custom_fusion = f32[10,64]{0,1:T(8,128)S(1)} fusion(s32[1024]{0:T(1024)S(1)} %bitcast.205, f32[1024,10]{1,0:T(8,128)S(1)} %copy.676, f32[]{:T(128)} %constant.342.clone.1), kind=kCustom, calls=%fused_computation.929 | custom fusion | flops 10240 | bytes 2564 | tf_op jit(solution)/shard_map/scatter-add | solution.py:86
  46.1 5.1 %collective-permute-start.9 = (f32[2,4,8,320]{3,2,1,0:T(8,128)S(1)}, f32[2,4,8,320]{3,2,1,0:T(8,128)S(1)}, u32[]{:S(2)}, u32[]{:S(2)}) collective-permute-start(f32[2,4,8,320]{3,2,1,0:T(8,128)S(1)} %get-tuple-element.249), channel_id=1, source_target_pairs={{4,0},{8,4},{12,8},{5,1},{9,5},{13,9},{6,2},{10,6},{14,10},{7,3},{... | collective-permute-start | bytes 245768 | tf_op jit(solution)/shard_map/ppermute | solution.py:17
  53.4 4.3 %collective-permute-done.8 = f32[2,4,8,320]{3,2,1,0:T(8,128)S(1)} collective-permute-done((f32[2,4,8,320]{3,2,1,0:T(8,128)S(1)}, f32[2,4,8,320]{3,2,1,0:T(8,128)S(1)}, u32[]{:S(2)}, u32[]{:S(2)}) %collective-permute-start.8) | collective-permute-done | bytes 81952 | tf_op jit(solution)/shard_map/ppermute | solution.py:14
  59.8 2.4 collective-permute-start.10
  63.1 3.8 %collective-permute-done.10 = f32[2,16,4,320]{3,1,2,0:T(8,128)S(1)} collective-permute-done((f32[2,16,4,320]{3,1,2,0:T(8,128)S(1)}, f32[2,16,4,320]{3,1,2,0:T(8,128)S(1)}, u32[]{:S(2)}, u32[]{:S(2)}) %collective-permute-start.10) | collective-permute-done | bytes 163872 | tf_op jit(solution)/shard_map/ppermute | solution.py:14
  70.5 3.8 %collective-permute-start.12 = (f32[2,4,8,320]{3,2,1,0:T(8,128)S(1)}, f32[2,4,8,320]{3,2,1,0:T(8,128)S(1)}, u32[]{:S(2)}, u32[]{:S(2)}) collective-permute-start(f32[2,4,8,320]{3,2,1,0:T(8,128)S(1)} %get-tuple-element.246), channel_id=1, source_target_pairs={{0,4},{4,8},{8,12},{1,5},{5,9},{9,13},{2,6},{6,10},{10,14},{3,7},{... | collective-permute-start | bytes 245768 | tf_op jit(solution)/shard_map/ppermute | solution.py:14
  79.1 2.4 collective-permute-start.14
  82.3 3.8 %collective-permute-done.14 = f32[2,16,4,320]{3,1,2,0:T(8,128)S(1)} collective-permute-done((f32[2,16,4,320]{3,1,2,0:T(8,128)S(1)}, f32[2,16,4,320]{3,1,2,0:T(8,128)S(1)}, u32[]{:S(2)}, u32[]{:S(2)}) %collective-permute-start.14) | collective-permute-done | bytes 163872 | tf_op jit(solution)/shard_map/ppermute | solution.py:14
  89.7 3.9 %collective-permute-start.16 = (f32[2,4,8,320]{3,2,1,0:T(8,128)S(1)}, f32[2,4,8,320]{3,2,1,0:T(8,128)S(1)}, u32[]{:S(2)}, u32[]{:S(2)}) collective-permute-start(f32[2,4,8,320]{3,2,1,0:T(8,128)S(1)} %get-tuple-element.244), channel_id=1, source_target_pairs={{0,4},{4,8},{8,12},{1,5},{5,9},{9,13},{2,6},{6,10},{10,14},{3,7},{... | collective-permute-start | bytes 245768 | tf_op jit(solution)/shard_map/ppermute | solution.py:14
  98.3 2.4 collective-permute-start.18
  101.6 3.8 %collective-permute-done.18 = f32[2,16,4,320]{3,1,2,0:T(8,128)S(1)} collective-permute-done((f32[2,16,4,320]{3,1,2,0:T(8,128)S(1)}, f32[2,16,4,320]{3,1,2,0:T(8,128)S(1)}, u32[]{:S(2)}, u32[]{:S(2)}) %collective-permute-start.18) | collective-permute-done | bytes 163872 | tf_op jit(solution)/shard_map/ppermute | solution.py:14
  109.0 3.9 %collective-permute-start.20 = (f32[2,4,8,320]{3,2,1,0:T(8,128)S(1)}, f32[2,4,8,320]{3,2,1,0:T(8,128)S(1)}, u32[]{:S(2)}, u32[]{:S(2)}) collective-permute-start(f32[2,4,8,320]{3,2,1,0:T(8,128)S(1)} %get-tuple-element.242), channel_id=1, source_target_pairs={{0,4},{4,8},{8,12},{1,5},{5,9},{9,13},{2,6},{6,10},{10,14},{3,7},{... | collective-permute-start | bytes 245768 | tf_op jit(solution)/shard_map/ppermute | solution.py:14
  117.6 2.4 collective-permute-start.22
  120.8 3.8 %collective-permute-done.22 = f32[2,16,4,320]{3,1,2,0:T(8,128)S(1)} collective-permute-done((f32[2,16,4,320]{3,1,2,0:T(8,128)S(1)}, f32[2,16,4,320]{3,1,2,0:T(8,128)S(1)}, u32[]{:S(2)}, u32[]{:S(2)}) %collective-permute-start.22) | collective-permute-done | bytes 163872 | tf_op jit(solution)/shard_map/ppermute | solution.py:14
  128.3 3.9 %collective-permute-start.24 = (f32[2,4,8,320]{3,2,1,0:T(8,128)S(1)}, f32[2,4,8,320]{3,2,1,0:T(8,128)S(1)}, u32[]{:S(2)}, u32[]{:S(2)}) collective-permute-start(f32[2,4,8,320]{3,2,1,0:T(8,128)S(1)} %get-tuple-element.240), channel_id=1, source_target_pairs={{0,4},{4,8},{8,12},{1,5},{5,9},{9,13},{2,6},{6,10},{10,14},{3,7},{... | collective-permute-start | bytes 245768 | tf_op jit(solution)/shard_map/ppermute | solution.py:14
  136.8 2.6 %collective-permute-start.26 = (f32[2,16,4,320]{3,1,2,0:T(8,128)S(1)}, f32[2,16,4,320]{3,1,2,0:T(8,128)S(1)}, u32[]{:S(2)}, u32[]{:S(2)}) collective-permute-start(f32[2,16,4,320]{3,1,2,0:T(8,128)S(1)} %copy.733), channel_id=1, source_target_pairs={{0,1},{1,2},{2,3},{4,5},{5,6},{6,7},{8,9},{9,10},{10,11},{12,13},{... | collective-permute-start | bytes 491528 | tf_op jit(solution)/shard_map/ppermute | solution.py:14
  140.1 3.8 %collective-permute-done.26 = f32[2,16,4,320]{3,1,2,0:T(8,128)S(1)} collective-permute-done((f32[2,16,4,320]{3,1,2,0:T(8,128)S(1)}, f32[2,16,4,320]{3,1,2,0:T(8,128)S(1)}, u32[]{:S(2)}, u32[]{:S(2)}) %collective-permute-start.26) | collective-permute-done | bytes 163872 | tf_op jit(solution)/shard_map/ppermute | solution.py:14
  147.5 3.9 %collective-permute-start.28 = (f32[2,4,8,320]{3,2,1,0:T(8,128)S(1)}, f32[2,4,8,320]{3,2,1,0:T(8,128)S(1)}, u32[]{:S(2)}, u32[]{:S(2)}) collective-permute-start(f32[2,4,8,320]{3,2,1,0:T(8,128)S(1)} %get-tuple-element.238), channel_id=1, source_target_pairs={{0,4},{4,8},{8,12},{1,5},{5,9},{9,13},{2,6},{6,10},{10,14},{3,7},{... | collective-permute-start | bytes 245768 | tf_op jit(solution)/shard_map/ppermute | solution.py:14
  159.3 3.8 %collective-permute-done.30 = f32[2,16,4,320]{3,1,2,0:T(8,128)S(1)} collective-permute-done((f32[2,16,4,320]{3,1,2,0:T(8,128)S(1)}, f32[2,16,4,320]{3,1,2,0:T(8,128)S(1)}, u32[]{:S(2)}, u32[]{:S(2)}) %collective-permute-start.30) | collective-permute-done | bytes 163872 | tf_op jit(solution)/shard_map/ppermute | solution.py:14
  166.8 3.9 %collective-permute-start.32 = (f32[2,4,8,320]{3,2,1,0:T(8,128)S(1)}, f32[2,4,8,320]{3,2,1,0:T(8,128)S(1)}, u32[]{:S(2)}, u32[]{:S(2)}) collective-permute-start(f32[2,4,8,320]{3,2,1,0:T(8,128)S(1)} %get-tuple-element.236), channel_id=1, source_target_pairs={{0,4},{4,8},{8,12},{1,5},{5,9},{9,13},{2,6},{6,10},{10,14},{3,7},{... | collective-permute-start | bytes 245768 | tf_op jit(solution)/shard_map/ppermute | solution.py:14
  175.4 2.4 collective-permute-start.34
  178.6 3.8 %collective-permute-done.34 = f32[2,16,4,320]{3,1,2,0:T(8,128)S(1)} collective-permute-done((f32[2,16,4,320]{3,1,2,0:T(8,128)S(1)}, f32[2,16,4,320]{3,1,2,0:T(8,128)S(1)}, u32[]{:S(2)}, u32[]{:S(2)}) %collective-permute-start.34) | collective-permute-done | bytes 163872 | tf_op jit(solution)/shard_map/ppermute | solution.py:14
  186.0 3.9 %collective-permute-start.36 = (f32[2,4,8,320]{3,2,1,0:T(8,128)S(1)}, f32[2,4,8,320]{3,2,1,0:T(8,128)S(1)}, u32[]{:S(2)}, u32[]{:S(2)}) collective-permute-start(f32[2,4,8,320]{3,2,1,0:T(8,128)S(1)} %get-tuple-element.234), channel_id=1, source_target_pairs={{0,4},{4,8},{8,12},{1,5},{5,9},{9,13},{2,6},{6,10},{10,14},{3,7},{... | collective-permute-start | bytes 245768 | tf_op jit(solution)/shard_map/ppermute | solution.py:14
  197.8 3.8 %collective-permute-done.38 = f32[2,16,4,320]{3,1,2,0:T(8,128)S(1)} collective-permute-done((f32[2,16,4,320]{3,1,2,0:T(8,128)S(1)}, f32[2,16,4,320]{3,1,2,0:T(8,128)S(1)}, u32[]{:S(2)}, u32[]{:S(2)}) %collective-permute-start.38) | collective-permute-done | bytes 163872 | tf_op jit(solution)/shard_map/ppermute | solution.py:14
  205.4 3.9 %collective-permute-start.40 = (f32[2,4,8,320]{3,2,1,0:T(8,128)S(1)}, f32[2,4,8,320]{3,2,1,0:T(8,128)S(1)}, u32[]{:S(2)}, u32[]{:S(2)}) collective-permute-start(f32[2,4,8,320]{3,2,1,0:T(8,128)S(1)} %get-tuple-element.232), channel_id=1, source_target_pairs={{0,4},{4,8},{8,12},{1,5},{5,9},{9,13},{2,6},{6,10},{10,14},{3,7},{... | collective-permute-start | bytes 245768 | tf_op jit(solution)/shard_map/ppermute | solution.py:14
  234.4 3.6 %collective-permute-done.42 = f32[2,16,4,320]{3,1,2,0:T(8,128)S(1)} collective-permute-done((f32[2,16,4,320]{3,1,2,0:T(8,128)S(1)}, f32[2,16,4,320]{3,1,2,0:T(8,128)S(1)}, u32[]{:S(2)}, u32[]{:S(2)}) %collective-permute-start.42) | collective-permute-done | bytes 163872 | tf_op jit(solution)/shard_map/ppermute | solution.py:14
  241.3 7.0 %fusion.361 = (f32[8,8,320]{2,1,0:T(8,128)}, f32[8,8,320]{2,1,0:T(8,128)}) fusion(f32[8,8,320]{2,1,0:T(8,128)S(1)} %multiply_add_fusion.1, f32[8,8,320]{2,1,0:T(8,128)S(1)} %multiply_add_fusion.3, f32[8,8,320]{2,1,0:T(8,128)S(1)} %multiply_add_fusion.4, f32[8,8,320]{2,1,0:T(8,128)S(1)} %multiply_add_fusion.8, f32[8,8,320]{2,1,0:T(8,128)S(1)} %copy-done.8, ...), kind=kLoop, calls=%fused_computation.864 | loop fusion | flops 1228800 | bytes 1556530 | tf_op jit(solution)/shard_map/add | solution.py:124
  (243 shorter events, 102.4 us)
Async XLA Ops:
  1.5 30.2 %collective-permute-start.1 = (f32[2,4,8,320]{3,2,1,0:T(8,128)S(1)}, f32[2,4,8,320]{3,2,1,0:T(8,128)S(1)}, u32[]{:S(2)}, u32[]{:S(2)}) collective-permute-start(f32[2,4,8,320]{3,2,1,0:T(8,128)S(1)} %get-tuple-element.251), channel_id=1, source_target_pairs={{4,0},{8,4},{12,8},{5,1},{9,5},{13,9},{6,2},{10,6},{14,10},{7,3},{... | collective-permute-start | bytes 245768 | tf_op jit(solution)/shard_map/ppermute | solution.py:17
  3.9 27.8 %collective-permute-start = (f32[2,4,8,320]{3,2,1,0:T(8,128)S(1)}, f32[2,4,8,320]{3,2,1,0:T(8,128)S(1)}, u32[]{:S(2)}, u32[]{:S(2)}) collective-permute-start(f32[2,4,8,320]{3,2,1,0:T(8,128)S(1)} %get-tuple-element.250), channel_id=1, source_target_pairs={{0,4},{4,8},{8,12},{1,5},{5,9},{9,13},{2,6},{6,10},{10,14},{3,7},{... | collective-permute-start | bytes 245768 | tf_op jit(solution)/shard_map/ppermute | solution.py:14
  7.4 12.3 %collective-permute-start.4 = (f32[10,64]{1,0:T(8,128)S(1)}, f32[10,64]{1,0:T(8,128)S(1)}, u32[]{:S(2)}, u32[]{:S(2)}) collective-permute-start(f32[10,64]{1,0:T(8,128)S(1)} %copy-done.6), channel_id=1, source_target_pairs={{0,15},{1,0},{2,1},{3,2},{4,3},{5,4},{6,5},{7,6},{8,7},{9,8},{10,9... | collective-permute-start | bytes 7688 | tf_op jit(solution)/shard_map/ppermute | solution.py:72
  29.7 6.5 %collective-permute-start.7 = (f32[10,512]{1,0:T(8,128)S(1)}, f32[10,512]{1,0:T(8,128)S(1)}, u32[]{:S(2)}, u32[]{:S(2)}) collective-permute-start(f32[10,512]{1,0:T(8,128)S(1)} %pad_maximum_fusion.30), channel_id=1, source_target_pairs={{0,8},{1,9},{2,10},{3,11},{4,12},{5,13},{6,14},{7,15},{8,0},{9,1},... | collective-permute-start | bytes 61448 | tf_op jit(solution)/shard_map/ppermute | solution.py:72
  31.8 10.9 %collective-permute-start.3 = (f32[2,16,4,320]{3,1,2,0:T(8,128)S(1)}, f32[2,16,4,320]{3,1,2,0:T(8,128)S(1)}, u32[]{:S(2)}, u32[]{:S(2)}) collective-permute-start(f32[2,16,4,320]{3,1,2,0:T(8,128)S(1)} %copy.724), channel_id=1, source_target_pairs={{1,0},{2,1},{3,2},{5,4},{6,5},{7,6},{9,8},{10,9},{11,10},{13,12},{... | collective-permute-start | bytes 491528 | tf_op jit(solution)/shard_map/ppermute | solution.py:17
  33.8 9.0 %collective-permute-start.2 = (f32[2,16,4,320]{3,1,2,0:T(8,128)S(1)}, f32[2,16,4,320]{3,1,2,0:T(8,128)S(1)}, u32[]{:S(2)}, u32[]{:S(2)}) collective-permute-start(f32[2,16,4,320]{3,1,2,0:T(8,128)S(1)} %copy.723), channel_id=1, source_target_pairs={{0,1},{1,2},{2,3},{4,5},{5,6},{6,7},{8,9},{9,10},{10,11},{12,13},{... | collective-permute-start | bytes 491528 | tf_op jit(solution)/shard_map/ppermute | solution.py:14
  46.1 7.3 %collective-permute-start.9 = (f32[2,4,8,320]{3,2,1,0:T(8,128)S(1)}, f32[2,4,8,320]{3,2,1,0:T(8,128)S(1)}, u32[]{:S(2)}, u32[]{:S(2)}) collective-permute-start(f32[2,4,8,320]{3,2,1,0:T(8,128)S(1)} %get-tuple-element.249), channel_id=1, source_target_pairs={{4,0},{8,4},{12,8},{5,1},{9,5},{13,9},{6,2},{10,6},{14,10},{7,3},{... | collective-permute-start | bytes 245768 | tf_op jit(solution)/shard_map/ppermute | solution.py:17
  51.3 6.5 %collective-permute-start.8 = (f32[2,4,8,320]{3,2,1,0:T(8,128)S(1)}, f32[2,4,8,320]{3,2,1,0:T(8,128)S(1)}, u32[]{:S(2)}, u32[]{:S(2)}) collective-permute-start(f32[2,4,8,320]{3,2,1,0:T(8,128)S(1)} %get-tuple-element.248), channel_id=1, source_target_pairs={{0,4},{4,8},{8,12},{1,5},{5,9},{9,13},{2,6},{6,10},{10,14},{3,7},{... | collective-permute-start | bytes 245768 | tf_op jit(solution)/shard_map/ppermute | solution.py:14
  59.8 7.0 %collective-permute-start.10 = (f32[2,16,4,320]{3,1,2,0:T(8,128)S(1)}, f32[2,16,4,320]{3,1,2,0:T(8,128)S(1)}, u32[]{:S(2)}, u32[]{:S(2)}) collective-permute-start(f32[2,16,4,320]{3,1,2,0:T(8,128)S(1)} %copy.725), channel_id=1, source_target_pairs={{0,1},{1,2},{2,3},{4,5},{5,6},{6,7},{8,9},{9,10},{10,11},{12,13},{... | collective-permute-start | bytes 491528 | tf_op jit(solution)/shard_map/ppermute | solution.py:14
  68.5 6.5 %collective-permute-start.13 = (f32[2,4,8,320]{3,2,1,0:T(8,128)S(1)}, f32[2,4,8,320]{3,2,1,0:T(8,128)S(1)}, u32[]{:S(2)}, u32[]{:S(2)}) collective-permute-start(f32[2,4,8,320]{3,2,1,0:T(8,128)S(1)} %get-tuple-element.247), channel_id=1, source_target_pairs={{4,0},{8,4},{12,8},{5,1},{9,5},{13,9},{6,2},{10,6},{14,10},{7,3},{... | collective-permute-start | bytes 245768 | tf_op jit(solution)/shard_map/ppermute | solution.py:17
  70.5 6.5 %collective-permute-start.12 = (f32[2,4,8,320]{3,2,1,0:T(8,128)S(1)}, f32[2,4,8,320]{3,2,1,0:T(8,128)S(1)}, u32[]{:S(2)}, u32[]{:S(2)}) collective-permute-start(f32[2,4,8,320]{3,2,1,0:T(8,128)S(1)} %get-tuple-element.246), channel_id=1, source_target_pairs={{0,4},{4,8},{8,12},{1,5},{5,9},{9,13},{2,6},{6,10},{10,14},{3,7},{... | collective-permute-start | bytes 245768 | tf_op jit(solution)/shard_map/ppermute | solution.py:14
  79.1 7.0 %collective-permute-start.14 = (f32[2,16,4,320]{3,1,2,0:T(8,128)S(1)}, f32[2,16,4,320]{3,1,2,0:T(8,128)S(1)}, u32[]{:S(2)}, u32[]{:S(2)}) collective-permute-start(f32[2,16,4,320]{3,1,2,0:T(8,128)S(1)} %copy.727), channel_id=1, source_target_pairs={{0,1},{1,2},{2,3},{4,5},{5,6},{6,7},{8,9},{9,10},{10,11},{12,13},{... | collective-permute-start | bytes 491528 | tf_op jit(solution)/shard_map/ppermute | solution.py:14
  87.8 6.5 %collective-permute-start.17 = (f32[2,4,8,320]{3,2,1,0:T(8,128)S(1)}, f32[2,4,8,320]{3,2,1,0:T(8,128)S(1)}, u32[]{:S(2)}, u32[]{:S(2)}) collective-permute-start(f32[2,4,8,320]{3,2,1,0:T(8,128)S(1)} %get-tuple-element.245), channel_id=1, source_target_pairs={{4,0},{8,4},{12,8},{5,1},{9,5},{13,9},{6,2},{10,6},{14,10},{7,3},{... | collective-permute-start | bytes 245768 | tf_op jit(solution)/shard_map/ppermute | solution.py:17
  89.7 6.5 %collective-permute-start.16 = (f32[2,4,8,320]{3,2,1,0:T(8,128)S(1)}, f32[2,4,8,320]{3,2,1,0:T(8,128)S(1)}, u32[]{:S(2)}, u32[]{:S(2)}) collective-permute-start(f32[2,4,8,320]{3,2,1,0:T(8,128)S(1)} %get-tuple-element.244), channel_id=1, source_target_pairs={{0,4},{4,8},{8,12},{1,5},{5,9},{9,13},{2,6},{6,10},{10,14},{3,7},{... | collective-permute-start | bytes 245768 | tf_op jit(solution)/shard_map/ppermute | solution.py:14
  98.3 7.0 %collective-permute-start.18 = (f32[2,16,4,320]{3,1,2,0:T(8,128)S(1)}, f32[2,16,4,320]{3,1,2,0:T(8,128)S(1)}, u32[]{:S(2)}, u32[]{:S(2)}) collective-permute-start(f32[2,16,4,320]{3,1,2,0:T(8,128)S(1)} %copy.729), channel_id=1, source_target_pairs={{0,1},{1,2},{2,3},{4,5},{5,6},{6,7},{8,9},{9,10},{10,11},{12,13},{... | collective-permute-start | bytes 491528 | tf_op jit(solution)/shard_map/ppermute | solution.py:14
  107.1 6.5 %collective-permute-start.21 = (f32[2,4,8,320]{3,2,1,0:T(8,128)S(1)}, f32[2,4,8,320]{3,2,1,0:T(8,128)S(1)}, u32[]{:S(2)}, u32[]{:S(2)}) collective-permute-start(f32[2,4,8,320]{3,2,1,0:T(8,128)S(1)} %get-tuple-element.243), channel_id=1, source_target_pairs={{4,0},{8,4},{12,8},{5,1},{9,5},{13,9},{6,2},{10,6},{14,10},{7,3},{... | collective-permute-start | bytes 245768 | tf_op jit(solution)/shard_map/ppermute | solution.py:17
  109.0 6.5 %collective-permute-start.20 = (f32[2,4,8,320]{3,2,1,0:T(8,128)S(1)}, f32[2,4,8,320]{3,2,1,0:T(8,128)S(1)}, u32[]{:S(2)}, u32[]{:S(2)}) collective-permute-start(f32[2,4,8,320]{3,2,1,0:T(8,128)S(1)} %get-tuple-element.242), channel_id=1, source_target_pairs={{0,4},{4,8},{8,12},{1,5},{5,9},{9,13},{2,6},{6,10},{10,14},{3,7},{... | collective-permute-start | bytes 245768 | tf_op jit(solution)/shard_map/ppermute | solution.py:14
  117.6 7.0 %collective-permute-start.22 = (f32[2,16,4,320]{3,1,2,0:T(8,128)S(1)}, f32[2,16,4,320]{3,1,2,0:T(8,128)S(1)}, u32[]{:S(2)}, u32[]{:S(2)}) collective-permute-start(f32[2,16,4,320]{3,1,2,0:T(8,128)S(1)} %copy.731), channel_id=1, source_target_pairs={{0,1},{1,2},{2,3},{4,5},{5,6},{6,7},{8,9},{9,10},{10,11},{12,13},{... | collective-permute-start | bytes 491528 | tf_op jit(solution)/shard_map/ppermute | solution.py:14
  126.3 6.5 %collective-permute-start.25 = (f32[2,4,8,320]{3,2,1,0:T(8,128)S(1)}, f32[2,4,8,320]{3,2,1,0:T(8,128)S(1)}, u32[]{:S(2)}, u32[]{:S(2)}) collective-permute-start(f32[2,4,8,320]{3,2,1,0:T(8,128)S(1)} %get-tuple-element.241), channel_id=1, source_target_pairs={{4,0},{8,4},{12,8},{5,1},{9,5},{13,9},{6,2},{10,6},{14,10},{7,3},{... | collective-permute-start | bytes 245768 | tf_op jit(solution)/shard_map/ppermute | solution.py:17
  128.3 6.5 %collective-permute-start.24 = (f32[2,4,8,320]{3,2,1,0:T(8,128)S(1)}, f32[2,4,8,320]{3,2,1,0:T(8,128)S(1)}, u32[]{:S(2)}, u32[]{:S(2)}) collective-permute-start(f32[2,4,8,320]{3,2,1,0:T(8,128)S(1)} %get-tuple-element.240), channel_id=1, source_target_pairs={{0,4},{4,8},{8,12},{1,5},{5,9},{9,13},{2,6},{6,10},{10,14},{3,7},{... | collective-permute-start | bytes 245768 | tf_op jit(solution)/shard_map/ppermute | solution.py:14
  136.8 7.0 %collective-permute-start.26 = (f32[2,16,4,320]{3,1,2,0:T(8,128)S(1)}, f32[2,16,4,320]{3,1,2,0:T(8,128)S(1)}, u32[]{:S(2)}, u32[]{:S(2)}) collective-permute-start(f32[2,16,4,320]{3,1,2,0:T(8,128)S(1)} %copy.733), channel_id=1, source_target_pairs={{0,1},{1,2},{2,3},{4,5},{5,6},{6,7},{8,9},{9,10},{10,11},{12,13},{... | collective-permute-start | bytes 491528 | tf_op jit(solution)/shard_map/ppermute | solution.py:14
  145.6 6.5 %collective-permute-start.29 = (f32[2,4,8,320]{3,2,1,0:T(8,128)S(1)}, f32[2,4,8,320]{3,2,1,0:T(8,128)S(1)}, u32[]{:S(2)}, u32[]{:S(2)}) collective-permute-start(f32[2,4,8,320]{3,2,1,0:T(8,128)S(1)} %get-tuple-element.239), channel_id=1, source_target_pairs={{4,0},{8,4},{12,8},{5,1},{9,5},{13,9},{6,2},{10,6},{14,10},{7,3},{... | collective-permute-start | bytes 245768 | tf_op jit(solution)/shard_map/ppermute | solution.py:17
  147.5 6.5 %collective-permute-start.28 = (f32[2,4,8,320]{3,2,1,0:T(8,128)S(1)}, f32[2,4,8,320]{3,2,1,0:T(8,128)S(1)}, u32[]{:S(2)}, u32[]{:S(2)}) collective-permute-start(f32[2,4,8,320]{3,2,1,0:T(8,128)S(1)} %get-tuple-element.238), channel_id=1, source_target_pairs={{0,4},{4,8},{8,12},{1,5},{5,9},{9,13},{2,6},{6,10},{10,14},{3,7},{... | collective-permute-start | bytes 245768 | tf_op jit(solution)/shard_map/ppermute | solution.py:14
  156.1 7.0 %collective-permute-start.30 = (f32[2,16,4,320]{3,1,2,0:T(8,128)S(1)}, f32[2,16,4,320]{3,1,2,0:T(8,128)S(1)}, u32[]{:S(2)}, u32[]{:S(2)}) collective-permute-start(f32[2,16,4,320]{3,1,2,0:T(8,128)S(1)} %copy.735), channel_id=1, source_target_pairs={{0,1},{1,2},{2,3},{4,5},{5,6},{6,7},{8,9},{9,10},{10,11},{12,13},{... | collective-permute-start | bytes 491528 | tf_op jit(solution)/shard_map/ppermute | solution.py:14
  164.9 6.5 %collective-permute-start.33 = (f32[2,4,8,320]{3,2,1,0:T(8,128)S(1)}, f32[2,4,8,320]{3,2,1,0:T(8,128)S(1)}, u32[]{:S(2)}, u32[]{:S(2)}) collective-permute-start(f32[2,4,8,320]{3,2,1,0:T(8,128)S(1)} %get-tuple-element.237), channel_id=1, source_target_pairs={{4,0},{8,4},{12,8},{5,1},{9,5},{13,9},{6,2},{10,6},{14,10},{7,3},{... | collective-permute-start | bytes 245768 | tf_op jit(solution)/shard_map/ppermute | solution.py:17
  166.8 6.5 %collective-permute-start.32 = (f32[2,4,8,320]{3,2,1,0:T(8,128)S(1)}, f32[2,4,8,320]{3,2,1,0:T(8,128)S(1)}, u32[]{:S(2)}, u32[]{:S(2)}) collective-permute-start(f32[2,4,8,320]{3,2,1,0:T(8,128)S(1)} %get-tuple-element.236), channel_id=1, source_target_pairs={{0,4},{4,8},{8,12},{1,5},{5,9},{9,13},{2,6},{6,10},{10,14},{3,7},{... | collective-permute-start | bytes 245768 | tf_op jit(solution)/shard_map/ppermute | solution.py:14
  175.4 7.0 %collective-permute-start.34 = (f32[2,16,4,320]{3,1,2,0:T(8,128)S(1)}, f32[2,16,4,320]{3,1,2,0:T(8,128)S(1)}, u32[]{:S(2)}, u32[]{:S(2)}) collective-permute-start(f32[2,16,4,320]{3,1,2,0:T(8,128)S(1)} %copy.737), channel_id=1, source_target_pairs={{0,1},{1,2},{2,3},{4,5},{5,6},{6,7},{8,9},{9,10},{10,11},{12,13},{... | collective-permute-start | bytes 491528 | tf_op jit(solution)/shard_map/ppermute | solution.py:14
  184.1 6.5 %collective-permute-start.37 = (f32[2,4,8,320]{3,2,1,0:T(8,128)S(1)}, f32[2,4,8,320]{3,2,1,0:T(8,128)S(1)}, u32[]{:S(2)}, u32[]{:S(2)}) collective-permute-start(f32[2,4,8,320]{3,2,1,0:T(8,128)S(1)} %get-tuple-element.235), channel_id=1, source_target_pairs={{4,0},{8,4},{12,8},{5,1},{9,5},{13,9},{6,2},{10,6},{14,10},{7,3},{... | collective-permute-start | bytes 245768 | tf_op jit(solution)/shard_map/ppermute | solution.py:17
  194.6 7.0 %collective-permute-start.38 = (f32[2,16,4,320]{3,1,2,0:T(8,128)S(1)}, f32[2,16,4,320]{3,1,2,0:T(8,128)S(1)}, u32[]{:S(2)}, u32[]{:S(2)}) collective-permute-start(f32[2,16,4,320]{3,1,2,0:T(8,128)S(1)} %copy.739), channel_id=1, source_target_pairs={{0,1},{1,2},{2,3},{4,5},{5,6},{6,7},{8,9},{9,10},{10,11},{12,13},{... | collective-permute-start | bytes 491528 | tf_op jit(solution)/shard_map/ppermute | solution.py:14
  203.4 25.6 %collective-permute-start.41 = (f32[2,4,8,320]{3,2,1,0:T(8,128)S(1)}, f32[2,4,8,320]{3,2,1,0:T(8,128)S(1)}, u32[]{:S(2)}, u32[]{:S(2)}) collective-permute-start(f32[2,4,8,320]{3,2,1,0:T(8,128)S(1)} %get-tuple-element.233), channel_id=1, source_target_pairs={{4,0},{8,4},{12,8},{5,1},{9,5},{13,9},{6,2},{10,6},{14,10},{7,3},{... | collective-permute-start | bytes 245768 | tf_op jit(solution)/shard_map/ppermute | solution.py:17
  205.4 23.6 %collective-permute-start.40 = (f32[2,4,8,320]{3,2,1,0:T(8,128)S(1)}, f32[2,4,8,320]{3,2,1,0:T(8,128)S(1)}, u32[]{:S(2)}, u32[]{:S(2)}) collective-permute-start(f32[2,4,8,320]{3,2,1,0:T(8,128)S(1)} %get-tuple-element.232), channel_id=1, source_target_pairs={{0,4},{4,8},{8,12},{1,5},{5,9},{9,13},{2,6},{6,10},{10,14},{3,7},{... | collective-permute-start | bytes 245768 | tf_op jit(solution)/shard_map/ppermute | solution.py:14
  231.1 7.0 %collective-permute-start.42 = (f32[2,16,4,320]{3,1,2,0:T(8,128)S(1)}, f32[2,16,4,320]{3,1,2,0:T(8,128)S(1)}, u32[]{:S(2)}, u32[]{:S(2)}) collective-permute-start(f32[2,16,4,320]{3,1,2,0:T(8,128)S(1)} %copy.741), channel_id=1, source_target_pairs={{0,1},{1,2},{2,3},{4,5},{5,6},{6,7},{8,9},{9,10},{10,11},{12,13},{... | collective-permute-start | bytes 491528 | tf_op jit(solution)/shard_map/ppermute | solution.py:14
  (26 other events, 216.9 us)
